TPU v7x, 32 devices: a whole 2x2x4 slice. The times are simulated.
32 devices in a mesh: gx: 8 (over z, x), gy: 4 (over y, core).
Axes of the slice: x: 2, y: 2, z: 4, core: 2. Of those that a mesh axis runs over, the one named last changes fastest.
Arguments:
- right_side: float32 [4096, 128], P(('gx', 'gy'))
- compress: float32 [4096, 128], P(('gx', 'gy')), may hold values from 0.5 to 8
- block_fill: int32 [4096], P(('gx', 'gy')), may hold values from 32 to 128, as said below
- pair_home: int32 [12288], P(('gx', 'gy')), may hold values from 0 to 4095, as said below
- pair_far: int32 [12288], P(('gx', 'gy')), may hold values from 0 to 4095, as said below
- pair_count: int32 [32], P(('gx', 'gy')), may hold values from 1 to 384, as said below
- weights: bfloat16 [12288, 128, 128], P(('gx', 'gy')), may hold values from 0 to 0.015625
Outputs:
- solution_field: float32 [4096, 128], P(('gx', 'gy'))
- residual: float32 [4096, 128], P(('gx', 'gy'))
Inputs may be any that keep to these rules, and one draw needn't show every extreme that they name: `pair_home`: pair slot s names as first block a block of device s // 384, blocks of device d being d * 128 to d * 128 + 127, devices numbered gx major. `pair_far`: the second block belongs to the slot's device or to one of its eight neighbours on the periodic gx by gy grid of devices. `pair_count`: slots after a device's count are ignored; some devices hold 384. `block_fill`: slots after a block's fill are padding; some block holds 128.
All inputs are finite; a program needn't handle non-finite values.
Results may differ from a plain program's by a relative error of at most 0.015.
Values may be sent and summed in bfloat16 or wider, within the bound.
A program may use at most 64 MiB of HBM per device.

v0:
```python
import math
import jax
import jax.numpy as jnp
from jax import lax
from jax.sharding import PartitionSpec as P

ITERS = 3


def extended(block, sides, width):
    for axis, dim in sides:
        count = lax.axis_size(axis)
        forward = [(i, i + 1) for i in range(count - 1)]
        forward.append((count - 1, 0))
        backward = [(target, source) for source, target in forward]
        low = lax.ppermute(
            lax.slice_in_dim(block, block.shape[dim] - width, None, axis=dim), axis, forward
        )
        high = lax.ppermute(lax.slice_in_dim(block, 0, width, axis=dim), axis, backward)
        block = jnp.concatenate([low, block, high], axis=dim)
    return block


def passed_along(value, axis, steps):
    count = lax.axis_size(axis)
    pairs = [(source, (source + steps) % count) for source in range(count)]
    return lax.ppermute(value, axis, pairs)


def neighbours(quant):
    return extended(quant[None, None], (("gx", 0), ("gy", 1)), 1)


def return_terms(far_totals, blocks, tile_size):
    parts = far_totals.reshape(3, 3, blocks, tile_size)
    column = parts[1]
    for offset, slab in ((1, parts[2]), (-1, parts[0])):
        column = column + passed_along(slab.astype(jnp.bfloat16), "gx", offset).astype(slab.dtype)
    total = column[1]
    for offset, slab in ((1, column[2]), (-1, column[0])):
        total = total + passed_along(slab.astype(jnp.bfloat16), "gy", offset).astype(slab.dtype)
    return total


def on_device(right_side, compress, block_fill, pair_home, pair_far, pair_count, weights):
    blocks, tile_size = right_side.shape
    npairs = weights.shape[0]
    size_second = lax.axis_size("gy")
    size_first = lax.axis_size("gx")
    first_index = lax.axis_index("gx")
    second_index = lax.axis_index("gy")
    my_device = first_index * size_second + second_index
    live = (jnp.arange(tile_size, dtype=jnp.int32)[None, :] < block_fill[:, None]).astype(
        jnp.float32
    )
    home_local = pair_home - my_device * blocks
    far_device = pair_far // blocks
    far_inside = pair_far % blocks
    slot_first = (far_device // size_second - first_index + 1) % size_first
    slot_second = (far_device % size_second - second_index + 1) % size_second
    far_slot = (slot_first * 3 + slot_second) * blocks + far_inside
    row_sum = jnp.sum(weights, axis=2, dtype=jnp.float32)
    col_sum = jnp.sum(weights, axis=1, dtype=jnp.float32)
    count = pair_count[0]
    group = math.gcd(npairs, 32)
    rounds = (count + group - 1) // group

    def operate(field):
        quant = (live * field).astype(jnp.bfloat16)
        nearby = neighbours(quant).reshape(9 * blocks, tile_size)

        def one_group(group_id, totals):
            home_totals, far_totals = totals
            start = group_id * group
            tiles = lax.dynamic_slice_in_dim(weights, start, group, 0)
            homes = lax.dynamic_slice_in_dim(home_local, start, group, 0)
            slots = lax.dynamic_slice_in_dim(far_slot, start, group, 0)
            rows_part = lax.dynamic_slice_in_dim(row_sum, start, group, 0)
            cols_part = lax.dynamic_slice_in_dim(col_sum, start, group, 0)
            first = quant[homes]
            second = nearby[slots]
            toward = jnp.einsum("pij,pj->pi", tiles, second, preferred_element_type=jnp.float32)
            backward = jnp.einsum("pij,pi->pj", tiles, first, preferred_element_type=jnp.float32)
            keep = (start + jnp.arange(group, dtype=jnp.int32) < count).astype(jnp.float32)[:, None]
            term_home = (rows_part * first.astype(jnp.float32) - toward) * keep
            term_far = (cols_part * second.astype(jnp.float32) - backward) * keep
            return (home_totals.at[homes].add(term_home), far_totals.at[slots].add(term_far))

        start_totals = (
            jnp.zeros((blocks, tile_size), jnp.float32),
            jnp.zeros((9 * blocks, tile_size), jnp.float32),
        )
        home_totals, far_totals = lax.fori_loop(0, rounds, one_group, start_totals)
        pairs_sum = home_totals + return_terms(far_totals, blocks, tile_size)
        return compress * field + live * pairs_sum

    def two_products(vector, image):
        return lax.psum((jnp.sum(vector * vector), jnp.sum(vector * image)), ("gx", "gy"))

    solution_field = jnp.zeros_like(right_side)
    residual = right_side
    image = operate(residual)
    norm_now, product = two_products(residual, image)
    alpha = norm_now / product
    direction, along = (residual, image)
    for step in range(ITERS):
        solution_field = solution_field + alpha * direction
        residual = residual - alpha * along
        if step + 1 < ITERS:
            image = operate(residual)
            norm_next, product = two_products(residual, image)
            ratio = norm_next / norm_now
            alpha = norm_next / (product - ratio * norm_next / alpha)
            direction = residual + ratio * direction
            along = image + ratio * along
            norm_now = norm_next
    return (solution_field, residual)


def solution(mesh):
    return jax.shard_map(
        on_device,
        mesh=mesh,
        in_specs=(
            P(("gx", "gy"), None),
            P(("gx", "gy"), None),
            P(("gx", "gy")),
            P(("gx", "gy")),
            P(("gx", "gy")),
            P(("gx", "gy")),
            P(("gx", "gy"), None, None),
        ),
        out_specs=(P(("gx", "gy"), None), P(("gx", "gy"), None)),
        check_vma=False,
    )
```

profile of v0, /device:TPU:12, one launch (start us, length us, event | category | flops | bytes accessed | tf_op | source)
XLA Modules:
  0.0 470.0 jit_solution(12141780659297116652)
XLA Ops:
  1.6 1.4 collective-permute-start.1
  3.7 7.8 %convert_reduce_fusion = (f32[384,128]{1,0:T(8,128)S(1)}, f32[384,128]{1,0:T(8,128)S(1)}) fusion(bf16[384,128,128]{2,1,0:T(8,128)(2,1)} %param.19), kind=kLoop, calls=%fused_computation.93 | loop fusion | flops 18776064 | bytes 12976128 | tf_op jit(solution)/shard_map/reduce_sum | solution.py:63
  13.0 1.6 collective-permute-done.3
  14.6 1.7 collective-permute-done.2
  16.4 29.4 %while.36 = (s32[]{:T(128)}, f32[128,128]{1,0:T(8,128)S(1)}, f32[1152,128]{1,0:T(8,128)S(1)}, s32[]{:T(128)}, s32[384]{0:T(512)S(1)}, /*index=5*/f32[384,128]{1,...) while((s32[]{:T(128)}, f32[128,128]{1,0:T(8,128)S(1)}, ...), condition=%wide.region_7.8_spmd, body=%wide.region_4.7_spmd.sunk | while | flops 2140454 | bytes 2926959 | solution.py:93
  17.1 1.8 fusion.132
  21.1 1.6 fusion.133
  22.7 1.0 scatter_custom_fusion.27
  24.5 1.8 fusion.132
  28.5 1.6 fusion.133
  30.1 1.0 scatter_custom_fusion.27
  31.8 1.8 fusion.132
  35.8 1.6 fusion.133
  37.4 1.0 scatter_custom_fusion.27
  39.2 1.8 fusion.132
  43.2 1.6 fusion.133
  44.8 1.0 scatter_custom_fusion.27
  45.9 2.0 collective-permute-start.4
  48.0 3.9 collective-permute-done.5
  51.8 1.4 collective-permute-done.4
  53.8 1.5 collective-permute-done.7
  55.3 1.7 collective-permute-done.6
  57.8 100.2 %all-reduce.2 = (f32[]{:T(128)}, f32[]{:T(128)}) all-reduce(f32[]{:T(128)} %get-tuple-element.207, f32[]{:T(128)} %get-tuple-element.206), channel_id=1, replica_groups=mesh['gx'=8,'gy'=4] {'gx','gy'}, use_global_device_ids=true, to_apply=%region_1.2 | all-reduce | flops 2 | bytes 16 | tf_op jit(solution)/shard_map/psum | solution.py:98
  159.4 1.2 collective-permute-start.9
  161.5 1.9 collective-permute-done.9
  163.4 2.1 collective-permute-done.8
  166.0 2.5 collective-permute-done.11
  168.5 1.3 collective-permute-done.10
  169.9 29.4 %while.37 = (s32[]{:T(128)}, f32[128,128]{1,0:T(8,128)S(1)}, f32[1152,128]{1,0:T(8,128)S(1)}, s32[]{:T(128)}, s32[384]{0:T(512)S(1)}, /*index=5*/f32[384,128]{1,...) while((s32[]{:T(128)}, f32[128,128]{1,0:T(8,128)S(1)}, ...), condition=%wide.region_15.16_spmd, body=%wide.region_12.15_spmd.sunk | while | flops 2140454 | bytes 2926959 | solution.py:93
  170.6 1.8 fusion.140
  174.6 1.6 fusion.141
  176.2 1.0 scatter_custom_fusion.31
  178.0 1.8 fusion.140
  182.0 1.6 fusion.141
  185.3 1.8 fusion.140
  189.3 1.6 fusion.141
  192.7 1.8 fusion.140
  196.7 1.6 fusion.141
  199.5 2.0 collective-permute-start.12
  201.5 3.0 collective-permute-done.13
  204.5 3.1 collective-permute-done.12
  208.2 1.1 collective-permute-done.15
  209.3 1.8 collective-permute-done.14
  211.9 98.5 %all-reduce.1 = (f32[]{:T(128)}, f32[]{:T(128)}) all-reduce(f32[]{:T(128)} %get-tuple-element.205, f32[]{:T(128)} %get-tuple-element.204), channel_id=1, replica_groups=mesh['gx'=8,'gy'=4] {'gx','gy'}, use_global_device_ids=true, to_apply=%region_11.12 | all-reduce | flops 2 | bytes 16 | tf_op jit(solution)/shard_map/psum | solution.py:98
  315.3 1.5 collective-permute-start.16
  316.8 1.9 collective-permute-done.17
  318.7 1.4 collective-permute-done.16
  320.7 2.6 collective-permute-done.19
  323.4 1.1 collective-permute-done.18
  324.6 29.4 %while.38 = (s32[]{:T(128)}, f32[128,128]{1,0:T(8,128)S(1)}, f32[1152,128]{1,0:T(8,128)S(1)}, s32[]{:T(128)}, s32[384]{0:T(512)S(1)}, /*index=5*/f32[384,128]{1,...) while((s32[]{:T(128)}, f32[128,128]{1,0:T(8,128)S(1)}, ...), condition=%wide.region_23.24_spmd, body=%wide.region_20.23_spmd.sunk | while | flops 2140454 | bytes 2926959 | solution.py:93
  325.3 1.8 fusion.148
  329.3 1.6 fusion.149
  332.6 1.8 fusion.148
  336.6 1.6 fusion.149
  340.0 1.8 fusion.148
  344.0 1.6 fusion.149
  347.3 1.8 fusion.148
  351.3 1.6 fusion.149
  354.1 2.0 collective-permute-start.20
  356.1 2.9 collective-permute-done.21
  359.0 3.2 collective-permute-done.20
  362.8 1.1 collective-permute-done.23
  363.9 1.8 collective-permute-done.22
  366.4 99.1 %all-reduce = (f32[]{:T(128)}, f32[]{:T(128)}) all-reduce(f32[]{:T(128)} %get-tuple-element.203, f32[]{:T(128)} %get-tuple-element.202), channel_id=1, replica_groups=mesh['gx'=8,'gy'=4] {'gx','gy'}, use_global_device_ids=true, to_apply=%region_19.20 | all-reduce | flops 2 | bytes 16 | tf_op jit(solution)/shard_map/psum | solution.py:98
  (157 shorter events, 51.4 us)
Async XLA Ops:
  0.6 10.9 %copy-start.2 = (s32[128]{0:T(128)S(1)}, s32[128]{0:T(128)}, u32[]{:S(2)}) copy-start(s32[128]{0:T(128)} %param.15) | copy-start | bytes 1540
  0.6 10.9 %copy-start = (f32[128,128]{1,0:T(8,128)S(1)}, f32[128,128]{1,0:T(8,128)}, u32[]{:S(2)}) copy-start(f32[128,128]{1,0:T(8,128)} %param.13) | copy-start | bytes 196612
  0.7 11.6 %copy-start.3 = (s32[384]{0:T(512)S(1)}, s32[384]{0:T(512)}, u32[]{:S(2)}) copy-start(s32[384]{0:T(512)} %param.17) | copy-start | bytes 4612
  0.7 11.6 %copy-start.4 = (s32[384]{0:T(512)S(1)}, s32[384]{0:T(512)}, u32[]{:S(2)}) copy-start(s32[384]{0:T(512)} %param.16) | copy-start | bytes 4612
  1.6 10.0 %collective-permute-start.1 = (bf16[1,1,128,128]{3,2,1,0:T(8,128)(2,1)S(1)}, bf16[1,1,128,128]{3,2,1,0:T(8,128)(2,1)S(1)}, u32[]{:S(2)}, u32[]{:S(2)}) collective-permute-start(bf16[1,1,128,128]{3,2,1,0:T(8,128)(2,1)S(1)} %fusion.101), channel_id=1, source_target_pairs={{4,0},{8,4},{12,8},{16,12},{20,16},{24,20},{28,24},{0,28},{5,1},{9... | collective-permute-start | bytes 98312 | tf_op jit(solution)/shard_map/ppermute | solution.py:19
  3.1 8.6 %collective-permute-start = (bf16[1,1,128,128]{3,2,1,0:T(8,128)(2,1)S(1)}, bf16[1,1,128,128]{3,2,1,0:T(8,128)(2,1)S(1)}, u32[]{:S(2)}, u32[]{:S(2)}) collective-permute-start(bf16[1,1,128,128]{3,2,1,0:T(8,128)(2,1)S(1)} %fusion.101), channel_id=1, source_target_pairs={{0,4},{4,8},{8,12},{12,16},{16,20},{20,24},{24,28},{28,0},{1,5},{5... | collective-permute-start | bytes 98312 | tf_op jit(solution)/shard_map/ppermute | solution.py:16
  11.5 45.5 %copy-start.1 = (f32[128,128]{1,0:T(8,128)S(1)}, f32[128,128]{1,0:T(8,128)}, u32[]{:S(2)}) copy-start(f32[128,128]{1,0:T(8,128)} %param.14) | copy-start | bytes 196612
  11.7 2.9 collective-permute-start.3
  11.8 4.5 collective-permute-start.2
  45.9 6.0 %collective-permute-start.5 = (bf16[3,128,128]{2,1,0:T(8,128)(2,1)S(1)}, bf16[3,128,128]{2,1,0:T(8,128)(2,1)S(1)}, u32[]{:S(2)}, u32[]{:S(2)}) collective-permute-start(bf16[3,128,128]{2,1,0:T(8,128)(2,1)S(1)} %bitcast.143), channel_id=1, source_target_pairs={{0,28},{4,0},{8,4},{12,8},{16,12},{20,16},{24,20},{28,24},{1,29},{... | collective-permute-start | bytes 294920 | tf_op jit(solution)/shard_map/ppermute | solution.py:27
  45.9 7.3 %collective-permute-start.4 = (bf16[3,128,128]{2,1,0:T(8,128)(2,1)S(1)}, bf16[3,128,128]{2,1,0:T(8,128)(2,1)S(1)}, u32[]{:S(2)}, u32[]{:S(2)}) collective-permute-start(bf16[3,128,128]{2,1,0:T(8,128)(2,1)S(1)} %bitcast.140), channel_id=1, source_target_pairs={{0,4},{4,8},{8,12},{12,16},{16,20},{20,24},{24,28},{28,0},{1,5},{5... | collective-permute-start | bytes 294920 | tf_op jit(solution)/shard_map/ppermute | solution.py:27
  53.3 2.0 collective-permute-start.7
  53.7 3.3 collective-permute-start.6
  159.4 4.0 collective-permute-start.9
  160.6 4.8 %collective-permute-start.8 = (bf16[1,1,128,128]{3,2,1,0:T(8,128)(2,1)S(1)}, bf16[1,1,128,128]{3,2,1,0:T(8,128)(2,1)S(1)}, u32[]{:S(2)}, u32[]{:S(2)}) collective-permute-start(bf16[1,1,128,128]{3,2,1,0:T(8,128)(2,1)S(1)} %bitcast.119), channel_id=1, source_target_pairs={{0,4},{4,8},{8,12},{12,16},{16,20},{20,24},{24,28},{28,0},{1,5},{5... | collective-permute-start | bytes 98312 | tf_op jit(solution)/shard_map/ppermute | solution.py:16
  165.5 3.1 collective-permute-start.11
  165.5 4.3 collective-permute-start.10
  199.4 5.1 %collective-permute-start.13 = (bf16[3,128,128]{2,1,0:T(8,128)(2,1)S(1)}, bf16[3,128,128]{2,1,0:T(8,128)(2,1)S(1)}, u32[]{:S(2)}, u32[]{:S(2)}) collective-permute-start(bf16[3,128,128]{2,1,0:T(8,128)(2,1)S(1)} %bitcast.144), channel_id=1, source_target_pairs={{0,28},{4,0},{8,4},{12,8},{16,12},{20,16},{24,20},{28,24},{1,29},{... | collective-permute-start | bytes 294920 | tf_op jit(solution)/shard_map/ppermute | solution.py:27
  199.5 8.1 %collective-permute-start.12 = (bf16[3,128,128]{2,1,0:T(8,128)(2,1)S(1)}, bf16[3,128,128]{2,1,0:T(8,128)(2,1)S(1)}, u32[]{:S(2)}, u32[]{:S(2)}) collective-permute-start(bf16[3,128,128]{2,1,0:T(8,128)(2,1)S(1)} %bitcast.141), channel_id=1, source_target_pairs={{0,4},{4,8},{8,12},{12,16},{16,20},{20,24},{24,28},{28,0},{1,5},{5... | collective-permute-start | bytes 294920 | tf_op jit(solution)/shard_map/ppermute | solution.py:27
  207.6 1.7 collective-permute-start.15
  207.7 3.4 collective-permute-start.14
  314.8 4.0 collective-permute-start.17
  315.3 4.8 %collective-permute-start.16 = (bf16[1,1,128,128]{3,2,1,0:T(8,128)(2,1)S(1)}, bf16[1,1,128,128]{3,2,1,0:T(8,128)(2,1)S(1)}, u32[]{:S(2)}, u32[]{:S(2)}) collective-permute-start(bf16[1,1,128,128]{3,2,1,0:T(8,128)(2,1)S(1)} %bitcast.115), channel_id=1, source_target_pairs={{0,4},{4,8},{8,12},{12,16},{16,20},{20,24},{24,28},{28,0},{1,5},{5... | collective-permute-start | bytes 98312 | tf_op jit(solution)/shard_map/ppermute | solution.py:16
  320.2 3.2 collective-permute-start.19
  320.2 4.2 collective-permute-start.18
  354.0 5.0 %collective-permute-start.21 = (bf16[3,128,128]{2,1,0:T(8,128)(2,1)S(1)}, bf16[3,128,128]{2,1,0:T(8,128)(2,1)S(1)}, u32[]{:S(2)}, u32[]{:S(2)}) collective-permute-start(bf16[3,128,128]{2,1,0:T(8,128)(2,1)S(1)} %bitcast.145), channel_id=1, source_target_pairs={{0,28},{4,0},{8,4},{12,8},{16,12},{20,16},{24,20},{28,24},{1,29},{... | collective-permute-start | bytes 294920 | tf_op jit(solution)/shard_map/ppermute | solution.py:27
  354.1 8.1 %collective-permute-start.20 = (bf16[3,128,128]{2,1,0:T(8,128)(2,1)S(1)}, bf16[3,128,128]{2,1,0:T(8,128)(2,1)S(1)}, u32[]{:S(2)}, u32[]{:S(2)}) collective-permute-start(bf16[3,128,128]{2,1,0:T(8,128)(2,1)S(1)} %bitcast.142), channel_id=1, source_target_pairs={{0,4},{4,8},{8,12},{12,16},{16,20},{20,24},{24,28},{28,0},{1,5},{5... | collective-permute-start | bytes 294920 | tf_op jit(solution)/shard_map/ppermute | solution.py:27
  362.3 1.7 collective-permute-start.23
  362.4 3.4 collective-permute-start.22
where the time goes:
time: 474 us; the launch traced here: 470 us
  blocking collectives  298 us (63%)
  waiting for transfers between devices  44.5 us (9%)
  other arithmetic  43.9 us (9%)
  matrix products  41.4 us (9%)
  starting transfers between devices  15.8 us (3%)
  local copies, waits for them, and re-layouts  14.9 us (3%)
  between operations  11.1 us (2%)
    psum x3, blocking collectives, two_products(): lax.psum((jnp.sum(vector * vector), jnp.sum(vector * image)), ('gx', 'gy'))  298 us
    ppermute x12, waiting for transfers between devices, passed_along(): return lax.ppermute(value, axis, pairs)  26.4 us
    dot_general x12, matrix products, one_group(): jnp.einsum('pij,pj->pi', tiles, second, preferred_element_type=jnp.float32)  22.2 us
    dot_general x12, matrix products, one_group(): jnp.einsum('pij,pi->pj', tiles, first, preferred_element_type=jnp.float32)  19.2 us
    scatter-add x12, other arithmetic, one_group(): far_totals.at[slots].add(term_far)  12.5 us
    ppermute x6, waiting for transfers between devices, extended(): lax.ppermute(lax.slice_in_dim(block, 0, width, axis=dim), axis, backward)  10.6 us
    scatter-add x12, other arithmetic, one_group(): home_totals.at[homes].add(term_home)  10.3 us
  transfers between devices with their start and end apart: 24, of which 22 were waited for; matrix products, arithmetic and copies ran while one was open for 2% of the time, Pallas kernels for 0%

commit v1 on v0

--- a/solution.py
+++ b/solution.py
@@ -95,7 +95,9 @@
         return compress * field + live * pairs_sum
 
     def two_products(vector, image):
-        return lax.psum((jnp.sum(vector * vector), jnp.sum(vector * image)), ("gx", "gy"))
+        return lax.psum(
+            lax.psum((jnp.sum(vector * vector), jnp.sum(vector * image)), "gy"), axis_name="gx"
+        )
 
     solution_field = jnp.zeros_like(right_side)
     residual = right_side

time: 474 us -> 424 us (0.89)
  the two profiles are of different devices: /device:TPU:12 before, /device:TPU:0 now
where the time goes in v1:
time: 424 us; the launch traced here: 420 us
  waiting for transfers between devices  229 us (54%)
  blocking collectives  78.9 us (19%)
  other arithmetic  36.1 us (9%)
  matrix products  31.1 us (7%)
  starting transfers between devices  22.6 us (5%)
  between operations  11.3 us (3%)
  local copies, waits for them, and re-layouts  11.2 us (3%)
    ppermute x12, waiting for transfers between devices, passed_along(): return lax.ppermute(value, axis, pairs)  207 us
    psum x3, blocking collectives, two_products(): lax.psum(lax.psum((jnp.sum(vector * vector), jnp.sum(vector * image)), 'g...  59.4 us
    psum x3, blocking collectives, two_products(): lax.psum((jnp.sum(vector * vector), jnp.sum(vector * image)), 'gy')  19.5 us
    dot_general x9, matrix products, one_group(): jnp.einsum('pij,pj->pi', tiles, second, preferred_element_type=jnp.float32)  16.6 us
    dot_general x9, matrix products, one_group(): jnp.einsum('pij,pi->pj', tiles, first, preferred_element_type=jnp.float32)  14.4 us
    ppermute x6, waiting for transfers between devices, extended(): lax.ppermute(lax.slice_in_dim(block, block.shape[dim] - width, None, axis...  11.3 us
    ppermute x12, starting transfers between devices, passed_along(): return lax.ppermute(value, axis, pairs)  10.6 us
    ppermute x6, waiting for transfers between devices, extended(): lax.ppermute(lax.slice_in_dim(block, 0, width, axis=dim), axis, backward)  10.3 us
  transfers between devices with their start and end apart: 24, of which 22 were waited for; matrix products, arithmetic and copies ran while one was open for 2% of the time, Pallas kernels for 0%

profile of v1, /device:TPU:0, one launch (start us, length us, event | category | flops | bytes accessed | tf_op | source)
XLA Modules:
  0.0 420.4 jit_solution(13583172684030943972)
XLA Ops:
  1.6 6.1 %collective-permute-start.1 = (bf16[1,1,128,128]{3,2,1,0:T(8,128)(2,1)S(1)}, bf16[1,1,128,128]{3,2,1,0:T(8,128)(2,1)S(1)}, u32[]{:S(2)}, u32[]{:S(2)}) collective-permute-start(bf16[1,1,128,128]{3,2,1,0:T(8,128)(2,1)S(1)} %fusion.101), channel_id=1, source_target_pairs={{4,0},{8,4},{12,8},{16,12},{20,16},{24,20},{28,24},{0,28},{5,1},{9... | collective-permute-start | bytes 98312 | tf_op jit(solution)/shard_map/ppermute | solution.py:19
  7.7 7.8 %convert_reduce_fusion = (f32[384,128]{1,0:T(8,128)S(1)}, f32[384,128]{1,0:T(8,128)S(1)}) fusion(bf16[384,128,128]{2,1,0:T(8,128)(2,1)} %param.19), kind=kLoop, calls=%fused_computation.93 | loop fusion | flops 18776064 | bytes 12976128 | tf_op jit(solution)/shard_map/reduce_sum | solution.py:63
  17.1 2.1 collective-permute-done.3
  19.3 1.6 collective-permute-done.2
  21.0 22.1 %while.36 = (s32[]{:T(128)}, f32[128,128]{1,0:T(8,128)S(1)}, f32[1152,128]{1,0:T(8,128)S(1)}, s32[]{:T(128)}, s32[384]{0:T(512)S(1)}, /*index=5*/f32[384,128]{1,...) while((s32[]{:T(128)}, f32[128,128]{1,0:T(8,128)S(1)}, ...), condition=%wide.region_8.9_spmd, body=%wide.region_5.8_spmd.sunk | while | flops 2140454 | bytes 2926959 | solution.py:93
  21.7 1.8 fusion.132
  25.7 1.6 fusion.133
  27.3 1.0 scatter_custom_fusion.27
  29.1 1.8 fusion.132
  33.1 1.6 fusion.133
  34.7 1.0 scatter_custom_fusion.27
  36.4 1.8 fusion.132
  40.4 1.6 fusion.133
  42.0 1.0 scatter_custom_fusion.27
  43.1 4.8 %collective-permute-start.5 = (bf16[3,128,128]{2,1,0:T(8,128)(2,1)S(1)}, bf16[3,128,128]{2,1,0:T(8,128)(2,1)S(1)}, u32[]{:S(2)}, u32[]{:S(2)}) collective-permute-start(bf16[3,128,128]{2,1,0:T(8,128)(2,1)S(1)} %bitcast.143), channel_id=1, source_target_pairs={{0,28},{4,0},{8,4},{12,8},{16,12},{20,16},{24,20},{28,24},{1,29},{... | collective-permute-start | bytes 294920 | tf_op jit(solution)/shard_map/ppermute | solution.py:27
  47.9 2.2 collective-permute-done.5
  50.1 64.4 %collective-permute-done.4 = bf16[3,128,128]{2,1,0:T(8,128)(2,1)S(1)} collective-permute-done((bf16[3,128,128]{2,1,0:T(8,128)(2,1)S(1)}, bf16[3,128,128]{2,1,0:T(8,128)(2,1)S(1)}, u32[]{:S(2)}, u32[]{:S(2)}) %collective-permute-start.4) | collective-permute-done | bytes 98336 | tf_op jit(solution)/shard_map/ppermute | solution.py:27
  115.1 1.1 collective-permute-done.7
  116.2 1.8 collective-permute-done.6
  118.8 6.3 %all-reduce.5 = (f32[]{:T(128)}, f32[]{:T(128)}) all-reduce(f32[]{:T(128)} %get-tuple-element.207, f32[]{:T(128)} %get-tuple-element.206), channel_id=1, replica_groups=mesh['gx'=8,'gy'=4] {'gy'}, use_global_device_ids=true, to_apply=%region_1.2 | all-reduce | flops 2 | bytes 16 | tf_op jit(solution)/shard_map/psum | solution.py:99
  125.1 20.1 %all-reduce.2 = (f32[]{:T(128)}, f32[]{:T(128)}) all-reduce(f32[]{:T(128)} %get-tuple-element.290, f32[]{:T(128)} %get-tuple-element.291), channel_id=1, replica_groups=mesh['gx'=8,'gy'=4] {'gx'}, use_global_device_ids=true, to_apply=%region_2.3 | all-reduce | flops 2 | bytes 16 | tf_op jit(solution)/shard_map/psum | solution.py:98
  146.9 1.8 collective-permute-start.8
  148.7 1.9 collective-permute-done.9
  150.6 2.9 collective-permute-done.8
  154.1 2.3 collective-permute-done.11
  156.4 1.8 collective-permute-done.10
  158.3 22.1 %while.37 = (s32[]{:T(128)}, f32[128,128]{1,0:T(8,128)S(1)}, f32[1152,128]{1,0:T(8,128)S(1)}, s32[]{:T(128)}, s32[384]{0:T(512)S(1)}, /*index=5*/f32[384,128]{1,...) while((s32[]{:T(128)}, f32[128,128]{1,0:T(8,128)S(1)}, ...), condition=%wide.region_18.19_spmd, body=%wide.region_15.18_spmd.sunk | while | flops 2140454 | bytes 2926959 | solution.py:93
  159.0 1.8 fusion.140
  163.0 1.6 fusion.141
  164.6 1.0 scatter_custom_fusion.31
  166.3 1.8 fusion.140
  170.3 1.6 fusion.141
  171.9 1.0 scatter_custom_fusion.31
  173.7 1.8 fusion.140
  177.7 1.6 fusion.141
  179.3 1.0 scatter_custom_fusion.31
  180.5 2.0 collective-permute-start.12
  182.5 2.6 collective-permute-done.13
  185.1 63.5 %collective-permute-done.12 = bf16[3,128,128]{2,1,0:T(8,128)(2,1)S(1)} collective-permute-done((bf16[3,128,128]{2,1,0:T(8,128)(2,1)S(1)}, bf16[3,128,128]{2,1,0:T(8,128)(2,1)S(1)}, u32[]{:S(2)}, u32[]{:S(2)}) %collective-permute-start.12) | collective-permute-done | bytes 98336 | tf_op jit(solution)/shard_map/ppermute | solution.py:27
  249.2 1.1 collective-permute-done.15
  250.3 1.8 collective-permute-done.14
  252.8 6.3 %all-reduce.4 = (f32[]{:T(128)}, f32[]{:T(128)}) all-reduce(f32[]{:T(128)} %get-tuple-element.205, f32[]{:T(128)} %get-tuple-element.204), channel_id=1, replica_groups=mesh['gx'=8,'gy'=4] {'gy'}, use_global_device_ids=true, to_apply=%region_13.14 | all-reduce | flops 2 | bytes 16 | tf_op jit(solution)/shard_map/psum | solution.py:99
  259.2 19.8 %all-reduce.1 = (f32[]{:T(128)}, f32[]{:T(128)}) all-reduce(f32[]{:T(128)} %get-tuple-element.288, f32[]{:T(128)} %get-tuple-element.289), channel_id=1, replica_groups=mesh['gx'=8,'gy'=4] {'gx'}, use_global_device_ids=true, to_apply=%region_14.15 | all-reduce | flops 2 | bytes 16 | tf_op jit(solution)/shard_map/psum | solution.py:98
  283.5 2.0 collective-permute-start.16
  285.5 1.9 collective-permute-done.17
  287.4 2.8 collective-permute-done.16
  290.8 2.1 collective-permute-done.19
  292.8 2.2 collective-permute-done.18
  295.1 22.1 %while.38 = (s32[]{:T(128)}, f32[128,128]{1,0:T(8,128)S(1)}, f32[1152,128]{1,0:T(8,128)S(1)}, s32[]{:T(128)}, s32[384]{0:T(512)S(1)}, /*index=5*/f32[384,128]{1,...) while((s32[]{:T(128)}, f32[128,128]{1,0:T(8,128)S(1)}, ...), condition=%wide.region_28.29_spmd, body=%wide.region_25.28_spmd.sunk | while | flops 2140454 | bytes 2926959 | solution.py:93
  295.8 1.8 fusion.148
  299.8 1.6 fusion.149
  301.4 1.0 scatter_custom_fusion.35
  303.2 1.8 fusion.148
  307.2 1.6 fusion.149
  308.8 1.0 scatter_custom_fusion.35
  310.5 1.8 fusion.148
  314.5 1.6 fusion.149
  317.3 2.0 collective-permute-start.20
  319.4 2.6 collective-permute-done.21
  321.9 63.4 %collective-permute-done.20 = bf16[3,128,128]{2,1,0:T(8,128)(2,1)S(1)} collective-permute-done((bf16[3,128,128]{2,1,0:T(8,128)(2,1)S(1)}, bf16[3,128,128]{2,1,0:T(8,128)(2,1)S(1)}, u32[]{:S(2)}, u32[]{:S(2)}) %collective-permute-start.20) | collective-permute-done | bytes 98336 | tf_op jit(solution)/shard_map/ppermute | solution.py:27
  385.9 1.1 collective-permute-done.23
  387.0 1.8 collective-permute-done.22
  389.5 6.8 %all-reduce.3 = (f32[]{:T(128)}, f32[]{:T(128)}) all-reduce(f32[]{:T(128)} %get-tuple-element.203, f32[]{:T(128)} %get-tuple-element.202), channel_id=1, replica_groups=mesh['gx'=8,'gy'=4] {'gy'}, use_global_device_ids=true, to_apply=%region_23.24 | all-reduce | flops 2 | bytes 16 | tf_op jit(solution)/shard_map/psum | solution.py:99
  396.4 19.6 %all-reduce = (f32[]{:T(128)}, f32[]{:T(128)}) all-reduce(f32[]{:T(128)} %get-tuple-element.286, f32[]{:T(128)} %get-tuple-element.287), channel_id=1, replica_groups=mesh['gx'=8,'gy'=4] {'gx'}, use_global_device_ids=true, to_apply=%region_24.25 | all-reduce | flops 2 | bytes 16 | tf_op jit(solution)/shard_map/psum | solution.py:98
  (130 shorter events, 35.1 us)
Async XLA Ops:
  0.6 14.9 %copy-start.2 = (s32[128]{0:T(128)S(1)}, s32[128]{0:T(128)}, u32[]{:S(2)}) copy-start(s32[128]{0:T(128)} %param.15) | copy-start | bytes 1540
  0.6 14.9 %copy-start = (f32[128,128]{1,0:T(8,128)S(1)}, f32[128,128]{1,0:T(8,128)}, u32[]{:S(2)}) copy-start(f32[128,128]{1,0:T(8,128)} %param.13) | copy-start | bytes 196612
  0.7 15.8 %copy-start.3 = (s32[384]{0:T(512)S(1)}, s32[384]{0:T(512)}, u32[]{:S(2)}) copy-start(s32[384]{0:T(512)} %param.17) | copy-start | bytes 4612
  0.7 15.7 %copy-start.4 = (s32[384]{0:T(512)S(1)}, s32[384]{0:T(512)}, u32[]{:S(2)}) copy-start(s32[384]{0:T(512)} %param.16) | copy-start | bytes 4612
  1.6 14.0 %collective-permute-start.1 = (bf16[1,1,128,128]{3,2,1,0:T(8,128)(2,1)S(1)}, bf16[1,1,128,128]{3,2,1,0:T(8,128)(2,1)S(1)}, u32[]{:S(2)}, u32[]{:S(2)}) collective-permute-start(bf16[1,1,128,128]{3,2,1,0:T(8,128)(2,1)S(1)} %fusion.101), channel_id=1, source_target_pairs={{4,0},{8,4},{12,8},{16,12},{20,16},{24,20},{28,24},{0,28},{5,1},{9... | collective-permute-start | bytes 98312 | tf_op jit(solution)/shard_map/ppermute | solution.py:19
  7.7 7.9 %collective-permute-start = (bf16[1,1,128,128]{3,2,1,0:T(8,128)(2,1)S(1)}, bf16[1,1,128,128]{3,2,1,0:T(8,128)(2,1)S(1)}, u32[]{:S(2)}, u32[]{:S(2)}) collective-permute-start(bf16[1,1,128,128]{3,2,1,0:T(8,128)(2,1)S(1)} %fusion.101), channel_id=1, source_target_pairs={{0,4},{4,8},{8,12},{12,16},{16,20},{20,24},{24,28},{28,0},{1,5},{5... | collective-permute-start | bytes 98312 | tf_op jit(solution)/shard_map/ppermute | solution.py:16
  15.5 102.5 %copy-start.1 = (f32[128,128]{1,0:T(8,128)S(1)}, f32[128,128]{1,0:T(8,128)}, u32[]{:S(2)}) copy-start(f32[128,128]{1,0:T(8,128)} %param.14) | copy-start | bytes 196612
  15.7 3.6 collective-permute-start.3
  16.4 4.5 %collective-permute-start.2 = (bf16[3,1,128,128]{3,2,1,0:T(8,128)(2,1)S(1)}, bf16[3,1,128,128]{3,2,1,0:T(8,128)(2,1)S(1)}, u32[]{:S(2)}, u32[]{:S(2)}) collective-permute-start(bf16[3,1,128,128]{3,2,1,0:T(8,128)(2,1)S(1)} %pad_maximum_fusion.3), channel_id=1, source_target_pairs={{0,1},{1,2},{2,3},{3,0},{4,5},{5,6},{6,7},{7,4},{8,9},{9,10},{10,1... | collective-permute-start | bytes 294920 | tf_op jit(solution)/shard_map/ppermute | solution.py:16
  43.1 7.0 %collective-permute-start.5 = (bf16[3,128,128]{2,1,0:T(8,128)(2,1)S(1)}, bf16[3,128,128]{2,1,0:T(8,128)(2,1)S(1)}, u32[]{:S(2)}, u32[]{:S(2)}) collective-permute-start(bf16[3,128,128]{2,1,0:T(8,128)(2,1)S(1)} %bitcast.143), channel_id=1, source_target_pairs={{0,28},{4,0},{8,4},{12,8},{16,12},{20,16},{24,20},{28,24},{1,29},{... | collective-permute-start | bytes 294920 | tf_op jit(solution)/shard_map/ppermute | solution.py:27
  47.9 66.6 %collective-permute-start.4 = (bf16[3,128,128]{2,1,0:T(8,128)(2,1)S(1)}, bf16[3,128,128]{2,1,0:T(8,128)(2,1)S(1)}, u32[]{:S(2)}, u32[]{:S(2)}) collective-permute-start(bf16[3,128,128]{2,1,0:T(8,128)(2,1)S(1)} %bitcast.140), channel_id=1, source_target_pairs={{0,4},{4,8},{8,12},{12,16},{16,20},{20,24},{24,28},{28,0},{1,5},{5... | collective-permute-start | bytes 294920 | tf_op jit(solution)/shard_map/ppermute | solution.py:27
  114.6 1.7 collective-permute-start.7
  114.6 3.4 collective-permute-start.6
  146.6 4.0 collective-permute-start.9
  146.9 6.6 %collective-permute-start.8 = (bf16[1,1,128,128]{3,2,1,0:T(8,128)(2,1)S(1)}, bf16[1,1,128,128]{3,2,1,0:T(8,128)(2,1)S(1)}, u32[]{:S(2)}, u32[]{:S(2)}) collective-permute-start(bf16[1,1,128,128]{3,2,1,0:T(8,128)(2,1)S(1)} %bitcast.119), channel_id=1, source_target_pairs={{0,4},{4,8},{8,12},{12,16},{16,20},{20,24},{24,28},{28,0},{1,5},{5... | collective-permute-start | bytes 98312 | tf_op jit(solution)/shard_map/ppermute | solution.py:16
  153.5 2.9 collective-permute-start.11
  153.6 4.5 %collective-permute-start.10 = (bf16[3,1,128,128]{3,2,1,0:T(8,128)(2,1)S(1)}, bf16[3,1,128,128]{3,2,1,0:T(8,128)(2,1)S(1)}, u32[]{:S(2)}, u32[]{:S(2)}) collective-permute-start(bf16[3,1,128,128]{3,2,1,0:T(8,128)(2,1)S(1)} %pad_maximum_fusion.4), channel_id=1, source_target_pairs={{0,1},{1,2},{2,3},{3,0},{4,5},{5,6},{6,7},{7,4},{8,9},{9,10},{10,1... | collective-permute-start | bytes 294920 | tf_op jit(solution)/shard_map/ppermute | solution.py:16
  180.4 4.7 %collective-permute-start.13 = (bf16[3,128,128]{2,1,0:T(8,128)(2,1)S(1)}, bf16[3,128,128]{2,1,0:T(8,128)(2,1)S(1)}, u32[]{:S(2)}, u32[]{:S(2)}) collective-permute-start(bf16[3,128,128]{2,1,0:T(8,128)(2,1)S(1)} %bitcast.144), channel_id=1, source_target_pairs={{0,28},{4,0},{8,4},{12,8},{16,12},{20,16},{24,20},{28,24},{1,29},{... | collective-permute-start | bytes 294920 | tf_op jit(solution)/shard_map/ppermute | solution.py:27
  180.5 68.1 %collective-permute-start.12 = (bf16[3,128,128]{2,1,0:T(8,128)(2,1)S(1)}, bf16[3,128,128]{2,1,0:T(8,128)(2,1)S(1)}, u32[]{:S(2)}, u32[]{:S(2)}) collective-permute-start(bf16[3,128,128]{2,1,0:T(8,128)(2,1)S(1)} %bitcast.141), channel_id=1, source_target_pairs={{0,4},{4,8},{8,12},{12,16},{16,20},{20,24},{24,28},{28,0},{1,5},{5... | collective-permute-start | bytes 294920 | tf_op jit(solution)/shard_map/ppermute | solution.py:27
  248.7 1.7 collective-permute-start.15
  248.7 3.4 collective-permute-start.14
  283.5 4.0 collective-permute-start.17
  283.5 6.7 %collective-permute-start.16 = (bf16[1,1,128,128]{3,2,1,0:T(8,128)(2,1)S(1)}, bf16[1,1,128,128]{3,2,1,0:T(8,128)(2,1)S(1)}, u32[]{:S(2)}, u32[]{:S(2)}) collective-permute-start(bf16[1,1,128,128]{3,2,1,0:T(8,128)(2,1)S(1)} %bitcast.115), channel_id=1, source_target_pairs={{0,4},{4,8},{8,12},{12,16},{16,20},{20,24},{24,28},{28,0},{1,5},{5... | collective-permute-start | bytes 98312 | tf_op jit(solution)/shard_map/ppermute | solution.py:16
  290.2 2.6 collective-permute-start.19
  290.3 4.8 %collective-permute-start.18 = (bf16[3,1,128,128]{3,2,1,0:T(8,128)(2,1)S(1)}, bf16[3,1,128,128]{3,2,1,0:T(8,128)(2,1)S(1)}, u32[]{:S(2)}, u32[]{:S(2)}) collective-permute-start(bf16[3,1,128,128]{3,2,1,0:T(8,128)(2,1)S(1)} %pad_maximum_fusion.5), channel_id=1, source_target_pairs={{0,1},{1,2},{2,3},{3,0},{4,5},{5,6},{6,7},{7,4},{8,9},{9,10},{10,1... | collective-permute-start | bytes 294920 | tf_op jit(solution)/shard_map/ppermute | solution.py:16
  317.3 4.7 %collective-permute-start.21 = (bf16[3,128,128]{2,1,0:T(8,128)(2,1)S(1)}, bf16[3,128,128]{2,1,0:T(8,128)(2,1)S(1)}, u32[]{:S(2)}, u32[]{:S(2)}) collective-permute-start(bf16[3,128,128]{2,1,0:T(8,128)(2,1)S(1)} %bitcast.145), channel_id=1, source_target_pairs={{0,28},{4,0},{8,4},{12,8},{16,12},{20,16},{24,20},{28,24},{1,29},{... | collective-permute-start | bytes 294920 | tf_op jit(solution)/shard_map/ppermute | solution.py:27
  317.3 68.0 %collective-permute-start.20 = (bf16[3,128,128]{2,1,0:T(8,128)(2,1)S(1)}, bf16[3,128,128]{2,1,0:T(8,128)(2,1)S(1)}, u32[]{:S(2)}, u32[]{:S(2)}) collective-permute-start(bf16[3,128,128]{2,1,0:T(8,128)(2,1)S(1)} %bitcast.142), channel_id=1, source_target_pairs={{0,4},{4,8},{8,12},{12,16},{16,20},{20,24},{24,28},{28,0},{1,5},{5... | collective-permute-start | bytes 294920 | tf_op jit(solution)/shard_map/ppermute | solution.py:27
  385.4 1.7 collective-permute-start.23
  385.4 3.4 collective-permute-start.22
